TPU v7x, 256 devices: a whole 4x4x8 slice. The times are simulated.
256 devices in a mesh: tm: 8 (over y, core), space: 32 (over x, z).
Axes of the slice: x: 4, y: 4, z: 8, core: 2. Of those that a mesh axis runs over, the one named last changes fastest.
Arguments:
- snapshots: float32 [2048, 128, 1024], P('space', None, 'tm'), may hold values from -6 to 6
- land_mask: int32 [2048, 128], P('space'), may hold values 0 or 1
- taps_rows: float32 [6], replicated, may hold values from -2.5 to 2.5
- taps_cols: float32 [6], replicated, may hold values from -2.5 to 2.5
- probes: float32 [1024, 64, 128], P('space'), may hold values from -6 to 6
Outputs:
- basis: float32 [1024, 64, 128], P('space', None, 'tm')
- coefficients: float32 [128, 128], P('tm')
All inputs are finite; a program needn't handle non-finite values. No bound on the sum of `land_mask` on one device may be relied on, other than what follows from the above.
Results may differ from a plain program's by a relative error of at most 0.00028.
Values sent between devices are 32-bit elements; how exact they have to be, the bound alone decides.
A program may use at most 64 MiB of HBM per device.

v0:
```python
import jax
import jax.numpy as jnp
from jax import lax
from jax.sharding import PartitionSpec as P

SIGN_STEPS = 8
exact_dot = lax.Precision.HIGHEST


def padded_2(x, sides, width):
    for axis, dim in sides:
        size, length = (lax.axis_size(axis), x.shape[dim])
        up = [(i, (i + 1) % size) for i in range(size - 1)]
        down = [(j, i) for i, j in up]
        last = lax.slice_in_dim(x, length - width, length, axis=dim)
        initial = lax.slice_in_dim(x, 0, width, axis=dim)
        before = lax.ppermute(last, axis, up)
        after = lax.ppermute(initial, axis, down)
        x = jnp.concatenate([before, x, after], axis=dim)
    return x


def partner(block, axis, distance):
    count = lax.axis_size(axis)
    route = []
    for low in range(count):
        high = low | 1 << distance
        if high != low and high < count:
            route += [(low, high), (high, low)]
    return lax.ppermute(block, axis, route)


def band_matrix(tap_values, out_count, in_width, shift_by):
    row_ids = lax.broadcasted_iota(jnp.int32, (out_count, in_width), 0)
    col_ids = lax.broadcasted_iota(jnp.int32, (out_count, in_width), 1)
    tap_offset = col_ids - 2 * row_ids - shift_by
    band_table = jnp.zeros((out_count, in_width), jnp.float32)
    for tap_index in range(6):
        band_table = band_table + jnp.where(tap_offset == tap_index, tap_values[tap_index], 0.0)
    return band_table


def merge_level(paired):
    partial_gram = jnp.einsum("gra,grb->gab", paired, paired, precision=exact_dot)
    gram_total = lax.psum(partial_gram, "space")
    order_size = gram_total.shape[-1]
    identity = jnp.eye(order_size, dtype=jnp.float32)
    mean_eig = jnp.sum(gram_total * identity, axis=(1, 2)) / order_size
    shifted = gram_total - mean_eig[:, None, None] * identity
    norm_scale = jnp.sqrt(jnp.sum(shifted * shifted, axis=(1, 2)) + 1e-06)
    sign_iter = shifted / norm_scale[:, None, None]
    for sweep_index in range(SIGN_STEPS):
        square = jnp.einsum("gab,gbc->gac", sign_iter, sign_iter, precision=exact_dot)
        sign_iter = 1.5 * sign_iter - 0.5 * jnp.einsum(
            "gab,gbc->gac", sign_iter, square, precision=exact_dot
        )
    projector = 0.5 * (identity + sign_iter)
    half_order = order_size // 2
    combine = projector[:, :, :half_order] + projector[:, :, half_order:]
    return jnp.einsum("gra,gab->grb", paired, combine, precision=exact_dot)


def local(snapshots, land_mask, taps_rows, taps_cols, probes):
    rows_dev, cell_cols, columns = snapshots.shape
    ocean_field = snapshots * land_mask.astype(jnp.float32)[:, :, None]
    across = band_matrix(taps_cols, cell_cols // 2, cell_cols, -2)
    narrowed = jnp.einsum("jy,xys->xjs", across, ocean_field, precision=exact_dot)
    padded = padded_2(narrowed, (("space", 0),), 3)
    row_filter = band_matrix(taps_rows, rows_dev // 2, rows_dev + 6, 1)
    filtered = jnp.einsum("ip,pjs->ijs", row_filter, padded, precision=exact_dot)
    cell_rows = rows_dev // 2 * (cell_cols // 2)
    factor = filtered.reshape(cell_rows, columns)
    flat_probes = probes.reshape(cell_rows, probes.shape[2])
    levels = lax.axis_size("tm").bit_length() - 1
    position = lax.axis_index("tm")
    merged = factor
    for level_index in range(levels):
        partner_fac = partner(merged, "tm", level_index)
        is_upper = position >> level_index & 1 == 1
        lower_part = jnp.where(is_upper, partner_fac, merged)
        upper_part = jnp.where(is_upper, merged, partner_fac)
        merged = merge_level(jnp.concatenate([lower_part, upper_part], axis=1)[None])[0]
    width_dev = columns // lax.axis_size("tm")
    col_start = position * width_dev
    partial_coef = jnp.einsum("rs,rp->sp", merged, flat_probes, precision=exact_dot)
    coefficients = lax.psum(partial_coef, "space")
    basis_own = lax.dynamic_slice_in_dim(merged, col_start, width_dev, 1)
    coef_own = lax.dynamic_slice_in_dim(coefficients, col_start, width_dev, 0)
    return (basis_own.reshape(rows_dev // 2, cell_cols // 2, width_dev), coef_own)


def solution(mesh):
    placed = (P("space", None, "tm"), P("space", None), P(), P(), P("space", None, None))
    return jax.shard_map(
        local,
        mesh=mesh,
        in_specs=placed,
        out_specs=(P("space", None, "tm"), P("tm", None)),
        check_vma=False,
    )
```

profile of v0, /device:TPU:2, one launch (start us, length us, event | category | flops | bytes accessed | tf_op | source)
XLA Modules:
  0.0 723.5 jit_solution(15306966266729676532)
XLA Ops:
  7.2 1.5 fusion.267
  8.8 0.8 convert_element_type.22
  9.5 9.0 %fusion.11 = f32[64,64,128]{2,1,0:T(8,128)S(1)} fusion(f32[64,128,128]{2,1,0:T(8,128)} %param.5, f32[64,128]{1,0:T(8,128)S(1)} %convert_element_type.22, f32[]{:T(128)} %bitcast.12, f32[]{:T(128)} %bitcast.11, f32[]{:T(128)} %bitcast.10, f32[]{:T(128)} %bitcast.9, f32[]{:T(128)} %bitcast.8, f32[]{:T(128)} %bitcast.7, s32[64]{0:T(128)S(1)} %iota_multiply_fusion), kind=kOutput, calls=%fused_computation.15 | convolution fusion | flops 806510592 | bytes 6324504 | tf_op jit(solution)/shard_map/jy,xys->xjs/dot_general | solution.py:67
  18.6 3.8 collective-permute-start
  22.4 5.8 collective-permute-start.1
  28.3 0.7 fusion.266
  29.1 1.3 collective-permute-done.1
  30.8 6.5 fusion.2
  37.2 0.6 copy.9
  38.0 0.9 copy-done.3
  38.9 1.9 collective-permute-done.2
  40.7 1.7 broadcast_select_fusion.1
  42.4 4.2 fusion.14
  46.6 0.5 all-reduce.7.cloned.1.call-start
  47.1 145.3 %all-reduce.5.cloned.1.call-done = f32[1,256,256]{2,1,0:T(8,128)} async-done(((f32[1,256,256]{2,1,0:T(8,128)}), f32[1,256,256]{2,1,0:T(8,128)}) %all-reduce.5.cloned.1.call-update) | async-done | bytes 262160 | tf_op jit(solution)/shard_map/psum | solution.py:45
  192.4 1.6 select_reduce_fusion.2
  194.6 1.6 multiply_reduce_fusion.2
  197.0 1.4 fusion.141
  198.4 1.4 fusion.41
  200.2 0.4 fusion.42
  201.0 0.4 fusion.43
  201.8 0.4 fusion.44
  202.6 0.4 fusion.45
  203.3 0.4 fusion.46
  204.1 0.4 fusion.47
  204.9 0.4 fusion.50
  205.3 3.3 fusion.9
  208.6 1.5 collective-permute-start.3
  210.1 19.3 %collective-permute-done.3 = f32[2048,128]{0,1:T(8,128)} collective-permute-done((f32[2048,128]{0,1:T(8,128)}, f32[2048,128]{0,1:T(8,128)}, u32[]{:S(2)}, u32[]{:S(2)}) %collective-permute-start.3) | collective-permute-done | bytes 1048608 | tf_op jit(solution)/shard_map/ppermute | solution.py:30
  229.4 1.7 broadcast_select_fusion.3
  231.1 2.6 fusion.15
  233.9 141.9 %all-reduce.7.cloned.1.call-done = f32[1,256,256]{2,1,0:T(8,128)} async-done(((f32[1,256,256]{2,1,0:T(8,128)}), f32[1,256,256]{2,1,0:T(8,128)}) %all-reduce.7.cloned.1.call-update) | async-done | bytes 262160 | tf_op jit(solution)/shard_map/psum | solution.py:45
  375.8 1.6 select_reduce_fusion.1
  378.0 1.6 multiply_reduce_fusion.1
  380.4 1.4 fusion.117
  381.8 1.4 fusion.51
  383.6 0.4 fusion.52
  384.4 0.4 fusion.53
  385.2 0.4 fusion.54
  386.0 0.4 fusion.55
  386.7 0.4 fusion.56
  387.5 0.4 fusion.57
  388.3 0.4 fusion.60
  388.7 2.3 fusion.7
  391.0 3.0 collective-permute-start.4
  394.0 19.3 %collective-permute-done.4 = f32[2048,128]{0,1:T(8,128)} collective-permute-done((f32[2048,128]{0,1:T(8,128)}, f32[2048,128]{0,1:T(8,128)}, u32[]{:S(2)}, u32[]{:S(2)}) %collective-permute-start.4) | collective-permute-done | bytes 1048608 | tf_op jit(solution)/shard_map/ppermute | solution.py:30
  413.3 1.7 broadcast_select_fusion.5
  415.0 2.6 fusion.16
  417.9 141.8 %all-reduce.9.cloned.1.call-done = f32[1,256,256]{2,1,0:T(8,128)} async-done(((f32[1,256,256]{2,1,0:T(8,128)}), f32[1,256,256]{2,1,0:T(8,128)}) %all-reduce.9.cloned.1.call-update) | async-done | bytes 262160 | tf_op jit(solution)/shard_map/psum | solution.py:45
  559.7 1.6 select_reduce_fusion
  562.0 1.6 multiply_reduce_fusion
  564.3 1.4 fusion.93
  565.8 1.4 fusion.61
  568.4 0.4 fusion.63
  569.1 0.4 fusion.64
  569.9 0.4 fusion.65
  570.7 0.4 fusion.66
  571.5 0.4 fusion.67
  572.2 0.4 fusion.70
  572.7 1.3 fusion.5
  574.0 1.8 fusion.268
  575.9 0.9 copy.10
  576.8 138.7 %all-reduce.11.cloned.1.call-done = f32[128,128]{1,0:T(8,128)} async-done(((f32[128,128]{1,0:T(8,128)}), f32[128,128]{1,0:T(8,128)}) %all-reduce.11.cloned.1.call-update) | async-done | bytes 65552 | tf_op jit(solution)/shard_map/psum | solution.py:86
  715.5 1.3 constant_dynamic-slice_fusion
  (46 shorter events, 9.6 us)
Async XLA Ops:
  7.2 566.8 %copy-start = (f32[32,64,128]{2,1,0:T(8,128)S(1)}, f32[32,64,128]{2,1,0:T(8,128)}, u32[]{:S(2)}) copy-start(f32[32,64,128]{2,1,0:T(8,128)} %param.9) | copy-start | bytes 3145732
  7.2 185.2 %all-reduce.5.cloned.1.call-start = ((), (), s32[]{:S(2)}) async-start(), calls=%async_computation | async-start | bytes 524288 | tf_op jit(solution)/shard_map/psum | solution.py:45
  9.5 18.7 %copy-start.4 = (f32[6]{0:T(128)S(1)}, f32[6]{0:T(128)}, u32[]{:S(2)}) copy-start(f32[6]{0:T(128)} %param.7) | copy-start | bytes 76
  18.6 10.5 %collective-permute-start = (f32[3,64,128]{2,1,0:T(8,128)S(1)}, f32[3,64,128]{2,1,0:T(8,128)S(1)}, u32[]{:S(2)}, u32[]{:S(2)}) collective-permute-start(f32[3,64,128]{2,1,0:T(8,128)S(1)} %get-tuple-element.10), channel_id=1, source_target_pairs={{0,1},{1,2},{2,3},{3,4},{4,5},{5,6},{6,7},{7,8},{8,9},{9,10},{10,1... | collective-permute-start | bytes 294920 | tf_op jit(solution)/shard_map/ppermute | solution.py:17
  22.4 8.0 %collective-permute-start.1 = (f32[3,64,128]{2,1,0:T(8,128)S(1)}, f32[3,64,128]{2,1,0:T(8,128)S(1)}, u32[]{:S(2)}, u32[]{:S(2)}) collective-permute-start(f32[3,64,128]{2,1,0:T(8,128)S(1)} %get-tuple-element.11), channel_id=1, source_target_pairs={{1,0},{2,1},{3,2},{4,3},{5,4},{6,5},{7,6},{8,7},{9,8},{10,9},{11,1... | collective-permute-start | bytes 294920 | tf_op jit(solution)/shard_map/ppermute | solution.py:18
  37.8 1.0 copy-start.3
  37.9 2.9 collective-permute-start.2
  46.6 329.2 %all-reduce.7.cloned.1.call-start = ((), (), s32[]{:S(2)}) async-start(), calls=%async_computation.1 | async-start | bytes 524288 | tf_op jit(solution)/shard_map/psum | solution.py:45
  208.6 20.8 %collective-permute-start.3 = (f32[2048,128]{0,1:T(8,128)}, f32[2048,128]{0,1:T(8,128)}, u32[]{:S(2)}, u32[]{:S(2)}) collective-permute-start(f32[2048,128]{0,1:T(8,128)} %fusion.9), channel_id=1, source_target_pairs={{0,64},{64,0},{32,96},{96,32},{128,192},{192,128},{160,224},{224,1... | collective-permute-start | bytes 3145736 | tf_op jit(solution)/shard_map/ppermute | solution.py:30
  233.7 326.0 %all-reduce.9.cloned.1.call-start = ((), (), s32[]{:S(2)}) async-start(), calls=%async_computation.2 | async-start | bytes 524288 | tf_op jit(solution)/shard_map/psum | solution.py:45
  391.0 22.3 %collective-permute-start.4 = (f32[2048,128]{0,1:T(8,128)}, f32[2048,128]{0,1:T(8,128)}, u32[]{:S(2)}, u32[]{:S(2)}) collective-permute-start(f32[2048,128]{0,1:T(8,128)} %fusion.7), channel_id=1, source_target_pairs={{0,128},{128,0},{32,160},{160,32},{64,192},{192,64},{96,224},{224,... | collective-permute-start | bytes 3145736 | tf_op jit(solution)/shard_map/ppermute | solution.py:30
  415.0 150.7 %copy-start.1 = (f32[2048,128]{0,1:T(8,128)}, f32[2048,128]{0,1:T(8,128)S(1)}, u32[]{:S(2)}) copy-start(f32[2048,128]{0,1:T(8,128)S(1)} %get-tuple-element.5) | copy-start | bytes 3145732
  417.6 297.8 %all-reduce.11.cloned.1.call-start = ((), (), s32[]{:S(2)}) async-start(), calls=%async_computation.3 | async-start | bytes 131072 | tf_op jit(solution)/shard_map/psum | solution.py:86
  570.3 2.4 copy-start.2
Sparse Core Ops, SparseCore 0:
  46.7 145.6 all-reduce.4
  233.8 141.9 all-reduce.6
  417.7 141.9 all-reduce.8
  575.9 139.4 all-reduce.10
where the time goes:
time: 731 us; the launch traced here: 724 us
  waiting for transfers between devices  610 us (83%)
  matrix products  58.2 us (8%)
  between operations  18.6 us (3%)
  other arithmetic  15.7 us (2%)
  starting transfers between devices  15.3 us (2%)
    psum x3, waiting for transfers between devices, merge_level(): gram_total = lax.psum(partial_gram, 'space')  429 us
    psum x1, waiting for transfers between devices, local(): coefficients = lax.psum(partial_coef, 'space')  139 us
    ppermute x3, waiting for transfers between devices, partner(): return lax.ppermute(block, axis, route)  40.4 us
  transfers between devices with their start and end apart: 9, of which 9 were waited for; matrix products, arithmetic and copies ran while one was open for 0% of the time, Pallas kernels for 0%

commit v1 on v0

--- a/solution.py
+++ b/solution.py
@@ -42,7 +42,11 @@
 
 def merge_level(paired):
     partial_gram = jnp.einsum("gra,grb->gab", paired, paired, precision=exact_dot)
-    gram_total = lax.psum(partial_gram, "space")
+    gram_total = partial_gram
+    for hop in (1, 2, 4, 8, 16):
+        gram_total = gram_total + lax.ppermute(
+            gram_total, "space", [(dev, dev ^ hop) for dev in range(32)]
+        )
     order_size = gram_total.shape[-1]
     identity = jnp.eye(order_size, dtype=jnp.float32)
     mean_eig = jnp.sum(gram_total * identity, axis=(1, 2)) / order_size

time: 731 us -> 459 us (0.63)
  waiting for transfers between devices: 610 us -> 328 us
  starting transfers between devices: 15.3 us -> 36.8 us
  matrix products: 58.2 us -> 49.9 us
    psum x3 -> x0, waiting for transfers between devices: 429 us -> none  [merge_level(): gram_total = lax.psum(partial_gram, 'space')]
    ppermute x0 -> x15, waiting for transfers between devices: none -> 140 us  [merge_level(): lax.ppermute(gram_total, 'space', [(dev, dev ^ hop) for dev in range(32)])]
    ppermute x0 -> x15, starting transfers between devices: none -> 22.3 us  [merge_level(): lax.ppermute(gram_total, 'space', [(dev, dev ^ hop) for dev in range(32)])]
  transfers between devices with their start and end apart: 9 -> 21, of which waited for: 9 -> 21; matrix products, arithmetic and copies ran while one was open for 0% -> 0% of each run, Pallas kernels for 0% -> 0%
where the time goes in v1:
time: 459 us; the launch traced here: 450 us
  waiting for transfers between devices  328 us (71%)
  matrix products  49.9 us (11%)
  starting transfers between devices  36.8 us (8%)
  between operations  19 us (4%)
  other arithmetic  10.1 us (2%)
  local copies, waits for them, and re-layouts  6.03 us (1%)
    ppermute x15, waiting for transfers between devices, merge_level(): lax.ppermute(gram_total, 'space', [(dev, dev ^ hop) for dev in range(32)])  140 us
    psum x1, waiting for transfers between devices, local(): coefficients = lax.psum(partial_coef, 'space')  140 us
    ppermute x3, waiting for transfers between devices, partner(): return lax.ppermute(block, axis, route)  45.9 us
    ppermute x15, starting transfers between devices, merge_level(): lax.ppermute(gram_total, 'space', [(dev, dev ^ hop) for dev in range(32)])  22.3 us
    dot_general x24, matrix products, merge_level(): jnp.einsum('gab,gbc->gac', sign_iter, square, precision=exact_dot)  9.25 us
  transfers between devices with their start and end apart: 21, of which 21 were waited for; matrix products, arithmetic and copies ran while one was open for 0% of the time, Pallas kernels for 0%

profile of v1, /device:TPU:2, one launch (start us, length us, event | category | flops | bytes accessed | tf_op | source)
XLA Modules:
  0.0 449.8 jit_solution(5661989173621370735)
XLA Ops:
  7.2 1.6 fusion.270
  8.8 0.8 convert_element_type.22
  9.6 9.1 %fusion.11 = f32[64,64,128]{2,1,0:T(8,128)S(1)} fusion(f32[64,128,128]{2,1,0:T(8,128)} %param.5, f32[64,128]{1,0:T(8,128)S(1)} %convert_element_type.22, f32[]{:T(128)} %bitcast.12, f32[]{:T(128)} %bitcast.11, f32[]{:T(128)} %bitcast.10, f32[]{:T(128)} %bitcast.9, f32[]{:T(128)} %bitcast.8, f32[]{:T(128)} %bitcast.7, s32[64]{0:T(128)S(1)} %iota_multiply_fusion), kind=kOutput, calls=%fused_computation.15 | convolution fusion | flops 806510592 | bytes 6324504 | tf_op jit(solution)/shard_map/jy,xys->xjs/dot_general | solution.py:71
  18.7 3.8 collective-permute-start
  22.5 5.8 %collective-permute-start.1 = (f32[3,64,128]{2,1,0:T(8,128)S(1)}, f32[3,64,128]{2,1,0:T(8,128)S(1)}, u32[]{:S(2)}, u32[]{:S(2)}) collective-permute-start(f32[3,64,128]{2,1,0:T(8,128)S(1)} %get-tuple-element.17), channel_id=1, source_target_pairs={{1,0},{2,1},{3,2},{4,3},{5,4},{6,5},{7,6},{8,7},{9,8},{10,9},{11,1... | collective-permute-start | bytes 294920 | tf_op jit(solution)/shard_map/ppermute | solution.py:18
  28.3 0.7 fusion.269
  29.2 1.3 collective-permute-done.1
  30.8 6.5 %fusion.2 = f32[32,64,128]{2,0,1:T(8,128)S(1)} fusion(f32[70,64,128]{2,1,0:T(8,128)S(1)} %pad_maximum_fusion, f32[]{:T(128)} %bitcast.5, f32[]{:T(128)} %bitcast.4, f32[]{:T(128)} %bitcast.3, f32[]{:T(128)} %bitcast.2, f32[]{:T(128)} %bitcast.1, f32[]{:T(128)} %bitcast, s32[32]{0:T(128)S(1)} %iota_multiply_fusion.1), kind=kOutput, calls=%fused_computation.2 | convolution fusion | flops 220243520 | bytes 3342488 | tf_op jit(solution)/shard_map/ip,pjs->ijs/dot_general | solution.py:74
  37.3 0.6 copy.9
  38.1 0.9 copy-done.3
  38.9 1.9 collective-permute-done.2
  40.8 1.7 broadcast_select_fusion.1
  42.5 3.5 fusion.14
  46.0 0.5 collective-permute-start.3
  46.5 8.0 %collective-permute-done.3 = f32[1,256,256]{2,1,0:T(8,128)S(1)} collective-permute-done((f32[1,256,256]{2,1,0:T(8,128)S(1)}, f32[1,256,256]{2,1,0:T(8,128)S(1)}, u32[]{:S(2)}, u32[]{:S(2)}) %collective-permute-start.3) | collective-permute-done | bytes 262176 | tf_op jit(solution)/shard_map/ppermute | solution.py:47
  54.5 4.4 collective-permute-start.4
  58.9 11.6 %collective-permute-done.4 = f32[1,256,256]{2,1,0:T(8,128)S(1)} collective-permute-done((f32[1,256,256]{2,1,0:T(8,128)S(1)}, f32[1,256,256]{2,1,0:T(8,128)S(1)}, u32[]{:S(2)}, u32[]{:S(2)}) %collective-permute-start.4) | collective-permute-done | bytes 262176 | tf_op jit(solution)/shard_map/ppermute | solution.py:47
  70.6 2.9 collective-permute-start.5
  73.5 13.9 %collective-permute-done.5 = f32[1,256,256]{2,1,0:T(8,128)S(1)} collective-permute-done((f32[1,256,256]{2,1,0:T(8,128)S(1)}, f32[1,256,256]{2,1,0:T(8,128)S(1)}, u32[]{:S(2)}, u32[]{:S(2)}) %collective-permute-start.5) | collective-permute-done | bytes 262176 | tf_op jit(solution)/shard_map/ppermute | solution.py:47
  87.4 0.6 collective-permute-start.6
  88.0 7.7 %collective-permute-done.6 = f32[1,256,256]{2,1,0:T(8,128)S(1)} collective-permute-done((f32[1,256,256]{2,1,0:T(8,128)S(1)}, f32[1,256,256]{2,1,0:T(8,128)S(1)}, u32[]{:S(2)}, u32[]{:S(2)}) %collective-permute-start.6) | collective-permute-done | bytes 262176 | tf_op jit(solution)/shard_map/ppermute | solution.py:47
  95.8 2.7 collective-permute-start.7
  98.4 6.8 %collective-permute-done.7 = f32[1,256,256]{2,1,0:T(8,128)S(1)} collective-permute-done((f32[1,256,256]{2,1,0:T(8,128)S(1)}, f32[1,256,256]{2,1,0:T(8,128)S(1)}, u32[]{:S(2)}, u32[]{:S(2)}) %collective-permute-start.7) | collective-permute-done | bytes 262176 | tf_op jit(solution)/shard_map/ppermute | solution.py:47
  105.2 0.6 select_reduce_fusion.2
  106.5 0.7 multiply_reduce_fusion.2
  107.9 0.4 fusion.138
  108.3 0.4 multiply_subtract_fusion.2
  114.1 3.3 fusion.9
  117.4 1.6 collective-permute-start.8
  119.0 22.1 %collective-permute-done.8 = f32[2048,128]{0,1:T(8,128)} collective-permute-done((f32[2048,128]{0,1:T(8,128)}, f32[2048,128]{0,1:T(8,128)}, u32[]{:S(2)}, u32[]{:S(2)}) %collective-permute-start.8) | collective-permute-done | bytes 1048608 | tf_op jit(solution)/shard_map/ppermute | solution.py:30
  141.1 1.7 broadcast_select_fusion.3
  142.8 1.9 fusion.15
  144.8 6.4 %collective-permute-done.9 = f32[1,256,256]{2,1,0:T(8,128)S(1)} collective-permute-done((f32[1,256,256]{2,1,0:T(8,128)S(1)}, f32[1,256,256]{2,1,0:T(8,128)S(1)}, u32[]{:S(2)}, u32[]{:S(2)}) %collective-permute-start.9) | collective-permute-done | bytes 262176 | tf_op jit(solution)/shard_map/ppermute | solution.py:47
  151.2 2.8 collective-permute-start.10
  154.0 8.4 %collective-permute-done.10 = f32[1,256,256]{2,1,0:T(8,128)S(1)} collective-permute-done((f32[1,256,256]{2,1,0:T(8,128)S(1)}, f32[1,256,256]{2,1,0:T(8,128)S(1)}, u32[]{:S(2)}, u32[]{:S(2)}) %collective-permute-start.10) | collective-permute-done | bytes 262176 | tf_op jit(solution)/shard_map/ppermute | solution.py:47
  162.4 2.9 collective-permute-start.11
  165.3 13.0 %collective-permute-done.11 = f32[1,256,256]{2,1,0:T(8,128)S(1)} collective-permute-done((f32[1,256,256]{2,1,0:T(8,128)S(1)}, f32[1,256,256]{2,1,0:T(8,128)S(1)}, u32[]{:S(2)}, u32[]{:S(2)}) %collective-permute-start.11) | collective-permute-done | bytes 262176 | tf_op jit(solution)/shard_map/ppermute | solution.py:47
  178.3 0.6 collective-permute-start.12
  178.9 7.7 %collective-permute-done.12 = f32[1,256,256]{2,1,0:T(8,128)S(1)} collective-permute-done((f32[1,256,256]{2,1,0:T(8,128)S(1)}, f32[1,256,256]{2,1,0:T(8,128)S(1)}, u32[]{:S(2)}, u32[]{:S(2)}) %collective-permute-start.12) | collective-permute-done | bytes 262176 | tf_op jit(solution)/shard_map/ppermute | solution.py:47
  186.7 2.1 collective-permute-start.13
  188.8 6.8 %collective-permute-done.13 = f32[1,256,256]{2,1,0:T(8,128)S(1)} collective-permute-done((f32[1,256,256]{2,1,0:T(8,128)S(1)}, f32[1,256,256]{2,1,0:T(8,128)S(1)}, u32[]{:S(2)}, u32[]{:S(2)}) %collective-permute-start.13) | collective-permute-done | bytes 262176 | tf_op jit(solution)/shard_map/ppermute | solution.py:47
  195.6 0.6 select_reduce_fusion.1
  196.9 0.7 multiply_reduce_fusion.1
  198.7 0.4 multiply_subtract_fusion.1
  204.5 2.3 fusion.7
  206.9 3.2 collective-permute-start.14
  210.0 21.9 %collective-permute-done.14 = f32[2048,128]{0,1:T(8,128)S(1)} collective-permute-done((f32[2048,128]{0,1:T(8,128)}, f32[2048,128]{0,1:T(8,128)S(1)}, u32[]{:S(2)}, u32[]{:S(2)}) %collective-permute-start.14) | collective-permute-done | bytes 1048608 | tf_op jit(solution)/shard_map/ppermute | solution.py:30
  231.9 1.4 broadcast_select_fusion.5
  233.3 1.9 fusion.16
  235.3 6.4 %collective-permute-done.15 = f32[1,256,256]{2,1,0:T(8,128)S(1)} collective-permute-done((f32[1,256,256]{2,1,0:T(8,128)S(1)}, f32[1,256,256]{2,1,0:T(8,128)S(1)}, u32[]{:S(2)}, u32[]{:S(2)}) %collective-permute-start.15) | collective-permute-done | bytes 262176 | tf_op jit(solution)/shard_map/ppermute | solution.py:47
  242.0 21.3 %collective-permute-done.16 = f32[1,256,256]{2,1,0:T(8,128)S(1)} collective-permute-done((f32[1,256,256]{2,1,0:T(8,128)S(1)}, f32[1,256,256]{2,1,0:T(8,128)S(1)}, u32[]{:S(2)}, u32[]{:S(2)}) %collective-permute-start.16) | collective-permute-done | bytes 262176 | tf_op jit(solution)/shard_map/ppermute | solution.py:47
  263.4 10.3 %collective-permute-done.17 = f32[1,256,256]{2,1,0:T(8,128)S(1)} collective-permute-done((f32[1,256,256]{2,1,0:T(8,128)S(1)}, f32[1,256,256]{2,1,0:T(8,128)S(1)}, u32[]{:S(2)}, u32[]{:S(2)}) %collective-permute-start.17) | collective-permute-done | bytes 262176 | tf_op jit(solution)/shard_map/ppermute | solution.py:47
  273.7 0.5 collective-permute-start.18
  274.2 5.9 %collective-permute-done.18 = f32[1,256,256]{2,1,0:T(8,128)S(1)} collective-permute-done((f32[1,256,256]{2,1,0:T(8,128)S(1)}, f32[1,256,256]{2,1,0:T(8,128)S(1)}, u32[]{:S(2)}, u32[]{:S(2)}) %collective-permute-start.18) | collective-permute-done | bytes 262176 | tf_op jit(solution)/shard_map/ppermute | solution.py:47
  280.2 1.7 collective-permute-start.19
  282.0 6.2 %collective-permute-done.19 = f32[1,256,256]{2,1,0:T(8,128)S(1)} collective-permute-done((f32[1,256,256]{2,1,0:T(8,128)S(1)}, f32[1,256,256]{2,1,0:T(8,128)S(1)}, u32[]{:S(2)}, u32[]{:S(2)}) %collective-permute-start.19) | collective-permute-done | bytes 262176 | tf_op jit(solution)/shard_map/ppermute | solution.py:47
  288.2 0.6 select_reduce_fusion
  289.5 0.7 multiply_reduce_fusion
  291.3 0.4 multiply_subtract_fusion
  297.1 1.3 fusion.5
  298.5 1.8 fusion.271
  300.4 0.9 copy.10
  301.2 140.2 %all-reduce.2.cloned.1.call-done = f32[128,128]{1,0:T(8,128)} async-done(((f32[128,128]{1,0:T(8,128)}), f32[128,128]{1,0:T(8,128)}) %all-reduce.2.cloned.1.call-update) | async-done | bytes 65552 | tf_op jit(solution)/shard_map/psum | solution.py:90
  441.4 1.3 constant_dynamic-slice_fusion
  (79 shorter events, 18.5 us)
Async XLA Ops:
  7.2 291.3 %copy-start = (f32[32,64,128]{2,1,0:T(8,128)S(1)}, f32[32,64,128]{2,1,0:T(8,128)}, u32[]{:S(2)}) copy-start(f32[32,64,128]{2,1,0:T(8,128)} %param.9) | copy-start | bytes 3145732
  7.2 434.2 %all-reduce.2.cloned.1.call-start = ((), (), s32[]{:S(2)}) async-start(), calls=%async_computation | async-start | bytes 131072 | tf_op jit(solution)/shard_map/psum | solution.py:90
  9.5 18.8 %copy-start.4 = (f32[6]{0:T(128)S(1)}, f32[6]{0:T(128)}, u32[]{:S(2)}) copy-start(f32[6]{0:T(128)} %param.7) | copy-start | bytes 76
  18.7 10.5 %collective-permute-start = (f32[3,64,128]{2,1,0:T(8,128)S(1)}, f32[3,64,128]{2,1,0:T(8,128)S(1)}, u32[]{:S(2)}, u32[]{:S(2)}) collective-permute-start(f32[3,64,128]{2,1,0:T(8,128)S(1)} %get-tuple-element.16), channel_id=1, source_target_pairs={{0,1},{1,2},{2,3},{3,4},{4,5},{5,6},{6,7},{7,8},{8,9},{9,10},{10,1... | collective-permute-start | bytes 294920 | tf_op jit(solution)/shard_map/ppermute | solution.py:17
  22.5 8.0 %collective-permute-start.1 = (f32[3,64,128]{2,1,0:T(8,128)S(1)}, f32[3,64,128]{2,1,0:T(8,128)S(1)}, u32[]{:S(2)}, u32[]{:S(2)}) collective-permute-start(f32[3,64,128]{2,1,0:T(8,128)S(1)} %get-tuple-element.17), channel_id=1, source_target_pairs={{1,0},{2,1},{3,2},{4,3},{5,4},{6,5},{7,6},{8,7},{9,8},{10,9},{11,1... | collective-permute-start | bytes 294920 | tf_op jit(solution)/shard_map/ppermute | solution.py:18
  37.9 1.0 copy-start.3
  37.9 2.9 collective-permute-start.2
  46.0 8.4 %collective-permute-start.3 = (f32[1,256,256]{2,1,0:T(8,128)S(1)}, f32[1,256,256]{2,1,0:T(8,128)S(1)}, u32[]{:S(2)}, u32[]{:S(2)}) collective-permute-start(f32[1,256,256]{2,1,0:T(8,128)S(1)} %fusion.14), channel_id=1, source_target_pairs={{0,1},{1,0},{2,3},{3,2},{4,5},{5,4},{6,7},{7,6},{8,9},{9,8},{10,11... | collective-permute-start | bytes 786440 | tf_op jit(solution)/shard_map/ppermute | solution.py:47
  54.5 16.1 %collective-permute-start.4 = (f32[1,256,256]{2,1,0:T(8,128)S(1)}, f32[1,256,256]{2,1,0:T(8,128)S(1)}, u32[]{:S(2)}, u32[]{:S(2)}) collective-permute-start(f32[1,256,256]{2,1,0:T(8,128)S(1)} %add.123), channel_id=1, source_target_pairs={{0,2},{1,3},{2,0},{3,1},{4,6},{5,7},{6,4},{7,5},{8,10},{9,11},{10,... | collective-permute-start | bytes 786440 | tf_op jit(solution)/shard_map/ppermute | solution.py:47
  70.6 16.8 %collective-permute-start.5 = (f32[1,256,256]{2,1,0:T(8,128)S(1)}, f32[1,256,256]{2,1,0:T(8,128)S(1)}, u32[]{:S(2)}, u32[]{:S(2)}) collective-permute-start(f32[1,256,256]{2,1,0:T(8,128)S(1)} %add.124), channel_id=1, source_target_pairs={{0,4},{1,5},{2,6},{3,7},{4,0},{5,1},{6,2},{7,3},{8,12},{9,13},{10,... | collective-permute-start | bytes 786440 | tf_op jit(solution)/shard_map/ppermute | solution.py:47
  87.4 8.3 %collective-permute-start.6 = (f32[1,256,256]{2,1,0:T(8,128)S(1)}, f32[1,256,256]{2,1,0:T(8,128)S(1)}, u32[]{:S(2)}, u32[]{:S(2)}) collective-permute-start(f32[1,256,256]{2,1,0:T(8,128)S(1)} %add.125), channel_id=1, source_target_pairs={{0,8},{1,9},{2,10},{3,11},{4,12},{5,13},{6,14},{7,15},{8,0},{9,1},... | collective-permute-start | bytes 786440 | tf_op jit(solution)/shard_map/ppermute | solution.py:47
  95.8 9.4 %collective-permute-start.7 = (f32[1,256,256]{2,1,0:T(8,128)S(1)}, f32[1,256,256]{2,1,0:T(8,128)S(1)}, u32[]{:S(2)}, u32[]{:S(2)}) collective-permute-start(f32[1,256,256]{2,1,0:T(8,128)S(1)} %add.126), channel_id=1, source_target_pairs={{0,16},{1,17},{2,18},{3,19},{4,20},{5,21},{6,22},{7,23},{8,24},{9,... | collective-permute-start | bytes 786440 | tf_op jit(solution)/shard_map/ppermute | solution.py:47
  117.4 23.7 %collective-permute-start.8 = (f32[2048,128]{0,1:T(8,128)}, f32[2048,128]{0,1:T(8,128)}, u32[]{:S(2)}, u32[]{:S(2)}) collective-permute-start(f32[2048,128]{0,1:T(8,128)} %fusion.9), channel_id=1, source_target_pairs={{0,64},{64,0},{32,96},{96,32},{128,192},{192,128},{160,224},{224,1... | collective-permute-start | bytes 3145736 | tf_op jit(solution)/shard_map/ppermute | solution.py:30
  144.7 6.5 %collective-permute-start.9 = (f32[1,256,256]{2,1,0:T(8,128)S(1)}, f32[1,256,256]{2,1,0:T(8,128)S(1)}, u32[]{:S(2)}, u32[]{:S(2)}) collective-permute-start(f32[1,256,256]{2,1,0:T(8,128)S(1)} %fusion.15), channel_id=1, source_target_pairs={{0,1},{1,0},{2,3},{3,2},{4,5},{5,4},{6,7},{7,6},{8,9},{9,8},{10,11... | collective-permute-start | bytes 786440 | tf_op jit(solution)/shard_map/ppermute | solution.py:47
  151.2 11.2 %collective-permute-start.10 = (f32[1,256,256]{2,1,0:T(8,128)S(1)}, f32[1,256,256]{2,1,0:T(8,128)S(1)}, u32[]{:S(2)}, u32[]{:S(2)}) collective-permute-start(f32[1,256,256]{2,1,0:T(8,128)S(1)} %add.131), channel_id=1, source_target_pairs={{0,2},{1,3},{2,0},{3,1},{4,6},{5,7},{6,4},{7,5},{8,10},{9,11},{10,... | collective-permute-start | bytes 786440 | tf_op jit(solution)/shard_map/ppermute | solution.py:47
  162.4 15.9 %collective-permute-start.11 = (f32[1,256,256]{2,1,0:T(8,128)S(1)}, f32[1,256,256]{2,1,0:T(8,128)S(1)}, u32[]{:S(2)}, u32[]{:S(2)}) collective-permute-start(f32[1,256,256]{2,1,0:T(8,128)S(1)} %add.132), channel_id=1, source_target_pairs={{0,4},{1,5},{2,6},{3,7},{4,0},{5,1},{6,2},{7,3},{8,12},{9,13},{10,... | collective-permute-start | bytes 786440 | tf_op jit(solution)/shard_map/ppermute | solution.py:47
  178.3 8.3 %collective-permute-start.12 = (f32[1,256,256]{2,1,0:T(8,128)S(1)}, f32[1,256,256]{2,1,0:T(8,128)S(1)}, u32[]{:S(2)}, u32[]{:S(2)}) collective-permute-start(f32[1,256,256]{2,1,0:T(8,128)S(1)} %add.133), channel_id=1, source_target_pairs={{0,8},{1,9},{2,10},{3,11},{4,12},{5,13},{6,14},{7,15},{8,0},{9,1},... | collective-permute-start | bytes 786440 | tf_op jit(solution)/shard_map/ppermute | solution.py:47
  186.7 9.0 %collective-permute-start.13 = (f32[1,256,256]{2,1,0:T(8,128)S(1)}, f32[1,256,256]{2,1,0:T(8,128)S(1)}, u32[]{:S(2)}, u32[]{:S(2)}) collective-permute-start(f32[1,256,256]{2,1,0:T(8,128)S(1)} %add.134), channel_id=1, source_target_pairs={{0,16},{1,17},{2,18},{3,19},{4,20},{5,21},{6,22},{7,23},{8,24},{9,... | collective-permute-start | bytes 786440 | tf_op jit(solution)/shard_map/ppermute | solution.py:47
  206.9 25.1 %collective-permute-start.14 = (f32[2048,128]{0,1:T(8,128)}, f32[2048,128]{0,1:T(8,128)S(1)}, u32[]{:S(2)}, u32[]{:S(2)}) collective-permute-start(f32[2048,128]{0,1:T(8,128)} %fusion.7), channel_id=1, source_target_pairs={{0,128},{128,0},{32,160},{160,32},{64,192},{192,64},{96,224},{224,... | collective-permute-start | bytes 3145736 | tf_op jit(solution)/shard_map/ppermute | solution.py:30
  233.3 40.4 %copy-start.1 = (f32[2048,128]{0,1:T(8,128)}, f32[2048,128]{0,1:T(8,128)S(1)}, u32[]{:S(2)}) copy-start(f32[2048,128]{0,1:T(8,128)S(1)} %get-tuple-element.11) | copy-start | bytes 3145732
  235.2 6.5 %collective-permute-start.15 = (f32[1,256,256]{2,1,0:T(8,128)S(1)}, f32[1,256,256]{2,1,0:T(8,128)S(1)}, u32[]{:S(2)}, u32[]{:S(2)}) collective-permute-start(f32[1,256,256]{2,1,0:T(8,128)S(1)} %fusion.16), channel_id=1, source_target_pairs={{0,1},{1,0},{2,3},{3,2},{4,5},{5,4},{6,7},{7,6},{8,9},{9,8},{10,11... | collective-permute-start | bytes 786440 | tf_op jit(solution)/shard_map/ppermute | solution.py:47
  241.7 21.6 %collective-permute-start.16 = (f32[1,256,256]{2,1,0:T(8,128)S(1)}, f32[1,256,256]{2,1,0:T(8,128)S(1)}, u32[]{:S(2)}, u32[]{:S(2)}) collective-permute-start(f32[1,256,256]{2,1,0:T(8,128)S(1)} %add.139), channel_id=1, source_target_pairs={{0,2},{1,3},{2,0},{3,1},{4,6},{5,7},{6,4},{7,5},{8,10},{9,11},{10,... | collective-permute-start | bytes 786440 | tf_op jit(solution)/shard_map/ppermute | solution.py:47
  263.3 10.4 %collective-permute-start.17 = (f32[1,256,256]{2,1,0:T(8,128)S(1)}, f32[1,256,256]{2,1,0:T(8,128)S(1)}, u32[]{:S(2)}, u32[]{:S(2)}) collective-permute-start(f32[1,256,256]{2,1,0:T(8,128)S(1)} %add.140), channel_id=1, source_target_pairs={{0,4},{1,5},{2,6},{3,7},{4,0},{5,1},{6,2},{7,3},{8,12},{9,13},{10,... | collective-permute-start | bytes 786440 | tf_op jit(solution)/shard_map/ppermute | solution.py:47
  273.7 6.5 %collective-permute-start.18 = (f32[1,256,256]{2,1,0:T(8,128)S(1)}, f32[1,256,256]{2,1,0:T(8,128)S(1)}, u32[]{:S(2)}, u32[]{:S(2)}) collective-permute-start(f32[1,256,256]{2,1,0:T(8,128)S(1)} %add.141), channel_id=1, source_target_pairs={{0,8},{1,9},{2,10},{3,11},{4,12},{5,13},{6,14},{7,15},{8,0},{9,1},... | collective-permute-start | bytes 786440 | tf_op jit(solution)/shard_map/ppermute | solution.py:47
  280.2 8.0 %collective-permute-start.19 = (f32[1,256,256]{2,1,0:T(8,128)S(1)}, f32[1,256,256]{2,1,0:T(8,128)S(1)}, u32[]{:S(2)}, u32[]{:S(2)}) collective-permute-start(f32[1,256,256]{2,1,0:T(8,128)S(1)} %add.142), channel_id=1, source_target_pairs={{0,16},{1,17},{2,18},{3,19},{4,20},{5,21},{6,22},{7,23},{8,24},{9,... | collective-permute-start | bytes 786440 | tf_op jit(solution)/shard_map/ppermute | solution.py:47
  294.8 2.3 copy-start.2
Sparse Core Ops, SparseCore 0:
  300.4 141.0 all-reduce.1
